TPU v7x, 32 devices: a whole 2x2x4 slice. The times are simulated.
32 devices in a mesh: row: 4 (over y, x), col: 8 (over z, core).
Axes of the slice: x: 2, y: 2, z: 4, core: 2. Of those that a mesh axis runs over, the one named last changes fastest.
Arguments:
- features: bfloat16 [32768, 128], P(('row', 'col')), may hold values from -6 to 6
- pair_index: int32 [2, 4096], P(None, ('row', 'col')), may hold values from -1 to 63, as said below
- bins: int32 [4096, 128, 128], P(('row', 'col')), may hold values from 0 to 8, as said below
- plate_weight: bfloat16 [1024, 128], replicated, may hold values from -0.1875 to 0.1875
- tower_weight: bfloat16 [1024, 128], replicated, may hold values from -0.1875 to 0.1875
- norm_gain: float32 [128], replicated, may hold values from 0.1 to 1.9
- update_in: bfloat16 [256, 128], replicated, may hold values from -0.375 to 0.375
- update_out: bfloat16 [128, 128], replicated, may hold values from -0.5 to 0.5
Outputs:
- updated: bfloat16 [32768, 128], P(('row', 'col'))
Inputs may be any that keep to these rules, and one draw needn't show every extreme that they name: `pair_index`: row 0 is a cluster of the meeting device's plate (below 64), row 1 a cluster of its tower (below 32). The 128 slots of one meeting device hold its live pairs first and then -1 in both rows. No cluster pair is live twice on one device. Some device has all 128 slots live. `bins`: 8 marks an atom pair that is no neighbour.
All inputs are finite; a program needn't handle non-finite values.
Results may differ from a plain program's by a relative error of at most 0.008.
Values may be sent and summed in bfloat16 or wider, within the bound.
A program may use at most 128 MiB of HBM per device.

v0:
```python
import jax
import jax.numpy as jnp
from jax import lax
from jax.sharding import PartitionSpec as P

D = 128
CLUSTER = 128
BINS = 8


def block_basis(pair_index, bins, turn, group):
    start = turn * group
    plate_idx = lax.dynamic_slice_in_dim(pair_index[0], start, group)
    tower_idx = lax.dynamic_slice_in_dim(pair_index[1], start, group)
    block = lax.dynamic_slice_in_dim(bins, start, group, 0)
    live = plate_idx >= 0
    levels = jnp.arange(BINS, dtype=jnp.int32)
    basis = (
        (block[:, :, None, :] == levels[None, None, :, None]) & live[:, None, None, None]
    ).astype(jnp.bfloat16)
    return (jnp.maximum(plate_idx, 0), jnp.maximum(tower_idx, 0), basis)


def plate_side(basis, tower, tower_at, plate_weight):
    count = basis.shape[0]
    near_plate = jnp.einsum(
        "gakb,gbd->gakd", basis, tower[tower_at], preferred_element_type=jnp.float32
    ).astype(jnp.bfloat16)
    message = jnp.dot(
        near_plate.reshape(count * CLUSTER, BINS * D),
        plate_weight,
        preferred_element_type=jnp.float32,
    )
    return message.reshape(count, CLUSTER, D)


def tower_side(basis, plate, plate_at, tower_weight):
    count = basis.shape[0]
    near_tower = jnp.einsum(
        "gakb,gad->gbkd", basis, plate[plate_at], preferred_element_type=jnp.float32
    ).astype(jnp.bfloat16)
    message = jnp.dot(
        near_tower.reshape(count * CLUSTER, BINS * D),
        tower_weight,
        preferred_element_type=jnp.float32,
    )
    return message.reshape(count, CLUSTER, D)


def return_tower(tower_acc, own_rows):
    flat = tower_acc.reshape(-1, D)
    summed = lax.psum(flat.astype(jnp.bfloat16), "row").astype(jnp.float32)
    return lax.dynamic_slice_in_dim(summed, lax.axis_index("row") * own_rows, own_rows, 0)


def return_plate(plate_acc, own_rows):
    flat = plate_acc.reshape(-1, D)
    summed = lax.psum(flat.astype(jnp.bfloat16), "col").astype(jnp.float32)
    return lax.dynamic_slice_in_dim(summed, lax.axis_index("col") * own_rows, own_rows, 0)


def shards(
    features, pair_index, bins, plate_weight, tower_weight, norm_gain, update_in, update_out
):
    own_rows = features.shape[0]
    plate = lax.all_gather(features, "col", axis=0, tiled=True).reshape(-1, CLUSTER, D)
    tower = lax.all_gather(features, "row", axis=0, tiled=True).reshape(-1, CLUSTER, D)
    group = 8
    slots = bins.shape[0]
    turns = slots // group
    plate_zero = jnp.zeros((plate.shape[0], CLUSTER, D), jnp.float32)
    tower_zero = jnp.zeros((tower.shape[0], CLUSTER, D), jnp.float32)

    def tower_step(turn, tower_acc):
        plate_at, tower_at, basis = block_basis(pair_index, bins, turn, group)
        return tower_acc.at[tower_at].add(tower_side(basis, plate, plate_at, tower_weight))

    def plate_step(turn, plate_acc):
        plate_at, tower_at, basis = block_basis(pair_index, bins, turn, group)
        return plate_acc.at[plate_at].add(plate_side(basis, tower, tower_at, plate_weight))

    tower_acc = lax.fori_loop(0, turns, tower_step, tower_zero)
    tower_back = return_tower(tower_acc, own_rows)
    plate_acc = lax.fori_loop(0, turns, plate_step, plate_zero)
    plate_back = return_plate(plate_acc, own_rows)
    incoming = plate_back + tower_back
    scale = lax.rsqrt(jnp.mean(incoming * incoming, axis=1, keepdims=True) + 1e-06)
    normed = (incoming * scale * norm_gain[None, :]).astype(jnp.bfloat16)
    joined = jnp.concatenate([features, normed], axis=1)
    hidden = jax.nn.silu(jnp.dot(joined, update_in, preferred_element_type=jnp.float32)).astype(
        jnp.bfloat16
    )
    result = features.astype(jnp.float32) + jnp.dot(
        hidden, update_out, preferred_element_type=jnp.float32
    )
    return result.astype(jnp.bfloat16)


def solution(mesh):
    placed = (
        P(("row", "col"), None),
        P(None, ("row", "col")),
        P(("row", "col"), None, None),
        P(),
        P(),
        P(),
        P(),
        P(),
    )
    return jax.shard_map(
        shards, mesh=mesh, in_specs=placed, out_specs=P(("row", "col"), None), check_vma=False
    )
```

profile of v0, /device:TPU:0, one launch (start us, length us, event | category | flops | bytes accessed | tf_op | source)
XLA Modules:
  0.0 342.0 jit_solution(12358343995069311886)
XLA Ops:
  8.1 30.4 %all-gather.3.cloned.1.call-done = bf16[4096,128]{1,0:T(8,128)(2,1)} async-done(((bf16[1024,128]{1,0:T(8,128)(2,1)}), bf16[4096,128]{1,0:T(8,128)(2,1)}) %all-gather.3.cloned.1.call-update) | async-done | bytes 1048592 | tf_op jit(solution)/shard_map/all_gather | solution.py:67
  38.4 2.5 broadcast_in_dim.38
  40.9 126.6 %while.26 = (s32[]{:T(128)}, f32[64,128,128]{2,1,0:T(8,128)}, s32[2,128]{1,0:T(2,128)S(1)}, s32[128,128,128]{2,1,0:T(8,128)}, bf16[32,128,128]{2,1,0:T(8,128)(2,...) while((s32[]{:T(128)}, f32[64,128,128]{2,1,0:T(8,128)}, ...), condition=%wide.region_2.0_spmd, body=%wide.region_0.0_spmd.sunk | while | flops 540148736 | bytes 8919471 | solution.py:84
  41.0 1.8 gather_fusion
  46.0 2.7 scatter_fusion
  48.9 1.8 gather_fusion
  53.9 2.7 scatter_fusion
  56.7 1.8 gather_fusion
  61.8 2.7 scatter_fusion
  64.6 1.8 gather_fusion
  69.6 2.8 scatter_fusion
  72.5 1.8 gather_fusion
  77.6 2.8 scatter_fusion
  80.4 1.8 gather_fusion
  85.5 2.8 scatter_fusion
  88.3 1.8 gather_fusion
  93.4 2.8 scatter_fusion
  96.3 1.8 gather_fusion
  101.3 2.8 scatter_fusion
  104.2 1.8 gather_fusion
  109.2 2.8 scatter_fusion
  112.1 1.8 gather_fusion
  117.2 2.8 scatter_fusion
  125.1 2.8 scatter_fusion
  133.0 2.8 scatter_fusion
  140.9 2.8 scatter_fusion
  148.9 2.8 scatter_fusion
  156.8 2.8 scatter_fusion
  164.7 2.8 scatter_fusion
  167.5 3.9 %convert_element_type.54 = bf16[64,128,128]{2,1,0:T(8,128)(2,1)} convert(f32[64,128,128]{2,1,0:T(8,128)} %get-tuple-element.223) | non-fusion elementwise | flops 1048576 | bytes 6291456 | tf_op jit(solution)/shard_map/convert_element_type | solution.py:58
  172.4 105.5 %while.27 = (s32[]{:T(128)}, f32[32,128,128]{2,1,0:T(8,128)S(1)}, s32[2,128]{1,0:T(2,128)S(1)}, bf16[64,128,128]{2,1,0:T(8,128)(2,1)}, s32[128,128,128]{2,1,0:T(...) while((s32[]{:T(128)}, f32[32,128,128]{2,1,0:T(8,128)S(1)}, ...), condition=%wide.region_6.0_spmd, body=%wide.region_4.0_spmd.sunk | while | flops 540148736 | bytes 8919471 | solution.py:82
  172.5 2.2 gather_fusion.1
  179.0 2.2 gather_fusion.1
  185.6 2.2 gather_fusion.1
  192.2 2.2 gather_fusion.1
  198.9 2.2 gather_fusion.1
  205.4 2.2 gather_fusion.1
  212.0 2.2 gather_fusion.1
  218.6 2.2 gather_fusion.1
  225.2 2.2 gather_fusion.1
  231.8 2.2 gather_fusion.1
  238.4 2.2 gather_fusion.1
  245.0 2.2 gather_fusion.1
  251.6 2.2 gather_fusion.1
  258.2 2.2 gather_fusion.1
  264.8 2.2 gather_fusion.1
  271.4 2.2 gather_fusion.1
  279.1 52.6 %all-reduce.5.cloned.1.call-done = bf16[4096,128]{1,0:T(8,128)(2,1)} async-done(((bf16[4096,128]{1,0:T(8,128)(2,1)}), bf16[4096,128]{1,0:T(8,128)(2,1)}) %all-reduce.5.cloned.1.call-update) | async-done | bytes 1048592 | tf_op jit(solution)/shard_map/psum | solution.py:52
  (276 shorter events, 140.3 us)
Async XLA Ops:
  6.5 327.7 %copy-start = (bf16[256,128]{1,0:T(8,128)(2,1)S(1)}, bf16[256,128]{1,0:T(8,128)(2,1)}, u32[]{:S(2)}) copy-start(bf16[256,128]{1,0:T(8,128)(2,1)} %param.18) | copy-start | bytes 196612
  6.5 31.9 %all-gather.3.cloned.1.call-start = ((), (), s32[]{:S(2)}) async-start(), calls=%async_computation | async-start | bytes 1310720 | tf_op jit(solution)/shard_map/all_gather | solution.py:67
  7.3 164.2 %all-gather.5.cloned.1.call-start = ((), (), s32[]{:S(2)}) async-start(), calls=%async_computation.2 | async-start | bytes 2359296 | tf_op jit(solution)/shard_map/all_gather | solution.py:66
  8.0 271.1 %all-reduce.3.cloned.1.call-start = ((), (), s32[]{:S(2)}) async-start(), calls=%async_computation.1 | async-start | bytes 4194304 | tf_op jit(solution)/shard_map/psum | solution.py:58
  38.4 2.5 copy-start.1
  38.4 2.5 copy-start.4
  171.4 0.9 copy-start.2
  171.4 160.2 %all-reduce.5.cloned.1.call-start = ((), (), s32[]{:S(2)}) async-start(), calls=%async_computation.3 | async-start | bytes 2097152 | tf_op jit(solution)/shard_map/psum | solution.py:52
  277.8 55.1 %copy-start.5 = (f32[128]{0:T(128)S(1)}, f32[128]{0:T(128)}, u32[]{:S(2)}) copy-start(f32[128]{0:T(128)} %param.17) | copy-start | bytes 1540
  277.9 56.4 %copy-start.3 = (bf16[1024,128]{1,0:T(8,128)(2,1)S(1)}, bf16[1024,128]{1,0:T(8,128)(2,1)}, u32[]{:S(2)}) copy-start(bf16[1024,128]{1,0:T(8,128)(2,1)} %param.12) | copy-start | bytes 786436
  277.9 56.3 %copy-start.6 = (bf16[128,128]{1,0:T(8,128)(2,1)S(1)}, bf16[128,128]{1,0:T(8,128)(2,1)}, u32[]{:S(2)}) copy-start(bf16[128,128]{1,0:T(8,128)(2,1)} %param.19) | copy-start | bytes 98308
Sparse Core Ops, SparseCore 0:
  9.2 29.2 all-gather.2
  40.0 29.1 all-gather.4
  171.6 65.1 all-reduce.2
  279.2 52.4 all-reduce.4
where the time goes:
time: 346 us; the launch traced here: 342 us
  local copies, waits for them, and re-layouts  102 us (29%)
  waiting for transfers between devices  84.4 us (24%)
  other arithmetic  73.5 us (21%)
  matrix products  67 us (19%)
  between operations  13.2 us (4%)
    psum x1, waiting for transfers between devices, return_tower(): summed = lax.psum(flat.astype(jnp.bfloat16), 'row').astype(jnp.float32)  52.6 us
    scatter-add x16, other arithmetic, plate_step(): plate_acc.at[plate_at].add(plate_side(basis, tower, tower_at, plate_weight))  44.2 us
    gather x16, local copies, waits for them, and re-layouts, tower_side(): plate[plate_at]  35.2 us
    dynamic_slice x32, local copies, waits for them, and re-layouts, block_basis(): block = lax.dynamic_slice_in_dim(bins, start, group, 0)  34.4 us
    all_gather x1, waiting for transfers between devices, shards(): lax.all_gather(features, 'row', axis=0, tiled=True).reshape(-1, CLUSTER, D)  30.4 us
    gather x16, local copies, waits for them, and re-layouts, plate_side(): tower[tower_at]  29.2 us
    dot_general x16, matrix products, plate_side(): jnp.einsum('gakb,gbd->gakd', basis, tower[tower_at], preferred_element_ty...  20.9 us
    dot_general x16, matrix products, tower_side(): jnp.einsum('gakb,gad->gbkd', basis, plate[plate_at], preferred_element_ty...  20.8 us
  transfers between devices with their start and end apart: 4, of which 2 were waited for; matrix products, arithmetic and copies ran while one was open for 70% of the time, Pallas kernels for 0%

commit v1 on v0

--- a/solution.py
+++ b/solution.py
@@ -6,6 +6,11 @@
 D = 128
 CLUSTER = 128
 BINS = 8
+
+
+def summed_here(value, axis):
+    parts = lax.all_gather(value, axis)
+    return jnp.sum(parts, axis=0)
 
 
 def block_basis(pair_index, bins, turn, group):
@@ -49,7 +54,7 @@
 
 def return_tower(tower_acc, own_rows):
     flat = tower_acc.reshape(-1, D)
-    summed = lax.psum(flat.astype(jnp.bfloat16), "row").astype(jnp.float32)
+    summed = summed_here(flat.astype(jnp.bfloat16), "row").astype(jnp.float32)
     return lax.dynamic_slice_in_dim(summed, lax.axis_index("row") * own_rows, own_rows, 0)
 
 

time: 346 us -> 360 us (1.040)
  waiting for transfers between devices: 84.4 us -> 95.5 us
    psum x1, waiting for transfers between devices: 0.02 us -> 61.3 us  [return_plate(): summed = lax.psum(flat.astype(jnp.bfloat16), 'col').astype(jnp.float32)]
    psum x1 -> x0, waiting for transfers between devices: 52.6 us -> none  [return_tower(): summed = lax.psum(flat.astype(jnp.bfloat16), 'row').astype(jnp.float32)]
    all_gather x1, waiting for transfers between devices: 0.02 us -> 32.8 us  [shards(): lax.all_gather(features, 'col', axis=0, tiled=True).reshape(-1, CLUSTER, D)]
    all_gather x1, waiting for transfers between devices: 30.4 us -> 0.02 us  [shards(): lax.all_gather(features, 'row', axis=0, tiled=True).reshape(-1, CLUSTER, D)]
  transfers between devices with their start and end apart: 4 -> 4, of which waited for: 2 -> 2; matrix products, arithmetic and copies ran while one was open for 70% -> 68% of each run, Pallas kernels for 0% -> 0%
where the time goes in v1:
time: 360 us; the launch traced here: 356 us
  local copies, waits for them, and re-layouts  102 us (28%)
  waiting for transfers between devices  95.5 us (27%)
  other arithmetic  76.8 us (21%)
  matrix products  67 us (19%)
  between operations  13.3 us (4%)
    psum x1, waiting for transfers between devices, return_plate(): summed = lax.psum(flat.astype(jnp.bfloat16), 'col').astype(jnp.float32)  61.3 us
    scatter-add x16, other arithmetic, plate_step(): plate_acc.at[plate_at].add(plate_side(basis, tower, tower_at, plate_weight))  44.2 us
    gather x16, local copies, waits for them, and re-layouts, tower_side(): plate[plate_at]  35.1 us
    dynamic_slice x32, local copies, waits for them, and re-layouts, block_basis(): block = lax.dynamic_slice_in_dim(bins, start, group, 0)  34.4 us
    all_gather x1, waiting for transfers between devices, shards(): lax.all_gather(features, 'col', axis=0, tiled=True).reshape(-1, CLUSTER, D)  32.8 us
    gather x16, local copies, waits for them, and re-layouts, plate_side(): tower[tower_at]  29.2 us
    dot_general x16, matrix products, plate_side(): jnp.einsum('gakb,gbd->gakd', basis, tower[tower_at], preferred_element_ty...  20.9 us
    dot_general x16, matrix products, tower_side(): jnp.einsum('gakb,gad->gbkd', basis, plate[plate_at], preferred_element_ty...  20.8 us
  transfers between devices with their start and end apart: 4, of which 2 were waited for; matrix products, arithmetic and copies ran while one was open for 68% of the time, Pallas kernels for 0%

profile of v1, /device:TPU:0, one launch (start us, length us, event | category | flops | bytes accessed | tf_op | source)
XLA Modules:
  0.0 355.9 jit_solution(17244666833676168626)
XLA Ops:
  8.1 32.8 %all-gather.6.cloned.1.call-done = bf16[8192,128]{1,0:T(8,128)(2,1)} async-done(((bf16[1024,128]{1,0:T(8,128)(2,1)}), bf16[8192,128]{1,0:T(8,128)(2,1)}) %all-gather.6.cloned.1.call-update) | async-done | bytes 2097168 | tf_op jit(solution)/shard_map/all_gather | solution.py:71
  41.1 105.4 %while.27 = (s32[]{:T(128)}, f32[32,128,128]{2,1,0:T(8,128)S(1)}, s32[2,128]{1,0:T(2,128)S(1)}, bf16[64,128,128]{2,1,0:T(8,128)(2,1)}, s32[128,128,128]{2,1,0:T(...) while((s32[]{:T(128)}, f32[32,128,128]{2,1,0:T(8,128)S(1)}, ...), condition=%wide.region_6.0_spmd, body=%wide.region_4.0_spmd.sunk | while | flops 540148736 | bytes 8919471 | solution.py:87
  41.2 2.2 gather_fusion.1
  47.8 2.3 gather_fusion.1
  54.5 2.2 gather_fusion.1
  61.0 2.2 gather_fusion.1
  67.6 2.2 gather_fusion.1
  74.2 2.2 gather_fusion.1
  80.8 2.2 gather_fusion.1
  87.4 2.2 gather_fusion.1
  94.0 2.2 gather_fusion.1
  100.6 2.2 gather_fusion.1
  107.1 2.2 gather_fusion.1
  113.7 2.2 gather_fusion.1
  120.3 2.2 gather_fusion.1
  126.9 2.2 gather_fusion.1
  133.5 2.2 gather_fusion.1
  140.1 2.2 gather_fusion.1
  147.8 2.5 broadcast_in_dim.38
  150.3 126.6 %while.26 = (s32[]{:T(128)}, f32[64,128,128]{2,1,0:T(8,128)}, s32[2,128]{1,0:T(2,128)S(1)}, s32[128,128,128]{2,1,0:T(8,128)}, bf16[32,128,128]{2,1,0:T(8,128)(2,...) while((s32[]{:T(128)}, f32[64,128,128]{2,1,0:T(8,128)}, ...), condition=%wide.region_2.0_spmd, body=%wide.region_0.0_spmd.sunk | while | flops 540148736 | bytes 8919471 | solution.py:89
  150.4 1.8 gather_fusion
  155.4 2.9 scatter_fusion
  158.4 1.8 gather_fusion
  163.4 2.7 scatter_fusion
  166.2 1.8 gather_fusion
  171.3 2.6 scatter_fusion
  174.0 1.8 gather_fusion
  179.1 2.8 scatter_fusion
  182.0 1.8 gather_fusion
  187.0 2.8 scatter_fusion
  189.9 1.8 gather_fusion
  194.9 2.8 scatter_fusion
  197.8 1.8 gather_fusion
  202.8 2.8 scatter_fusion
  205.7 1.8 gather_fusion
  210.8 2.8 scatter_fusion
  213.6 1.8 gather_fusion
  218.7 2.8 scatter_fusion
  226.6 2.8 scatter_fusion
  234.5 2.8 scatter_fusion
  242.5 2.8 scatter_fusion
  250.4 2.8 scatter_fusion
  258.3 2.8 scatter_fusion
  266.2 2.8 scatter_fusion
  274.1 2.8 scatter_fusion
  276.9 3.9 %convert_element_type.63 = bf16[64,128,128]{2,1,0:T(8,128)(2,1)} convert(f32[64,128,128]{2,1,0:T(8,128)} %get-tuple-element.223) | non-fusion elementwise | flops 1048576 | bytes 6291456 | tf_op jit(solution)/shard_map/convert_element_type | solution.py:63
  280.9 3.5 reduce_sum.21
  284.4 61.3 %all-reduce.2.cloned.1.call-done = bf16[8192,128]{1,0:T(8,128)(2,1)} async-done(((bf16[8192,128]{1,0:T(8,128)(2,1)}), bf16[8192,128]{1,0:T(8,128)(2,1)}) %all-reduce.2.cloned.1.call-update) | async-done | bytes 2097168 | tf_op jit(solution)/shard_map/psum | solution.py:63
  (277 shorter events, 141.4 us)
Async XLA Ops:
  6.5 341.5 %copy-start = (bf16[256,128]{1,0:T(8,128)(2,1)S(1)}, bf16[256,128]{1,0:T(8,128)(2,1)}, u32[]{:S(2)}) copy-start(bf16[256,128]{1,0:T(8,128)(2,1)} %param.18) | copy-start | bytes 196612
  6.5 34.5 %copy-start.4 = (s32[2,128]{1,0:T(2,128)S(1)}, s32[2,128]{1,0:T(2,128)}, u32[]{:S(2)}) copy-start(s32[2,128]{1,0:T(2,128)} %param.13) | copy-start | bytes 3076
  6.5 34.6 %copy-start.1 = (bf16[1024,128]{1,0:T(8,128)(2,1)S(1)}, bf16[1024,128]{1,0:T(8,128)(2,1)}, u32[]{:S(2)}) copy-start(bf16[1024,128]{1,0:T(8,128)(2,1)} %param.16) | copy-start | bytes 786436
  6.5 34.3 %all-gather.6.cloned.1.call-start = ((), (), s32[]{:S(2)}) async-start(), calls=%async_computation.2 | async-start | bytes 2359296 | tf_op jit(solution)/shard_map/all_gather | solution.py:71
  7.3 140.5 %all-gather.4.cloned.1.call-start = ((), (), s32[]{:S(2)}) async-start(), calls=%async_computation | async-start | bytes 1310720 | tf_op jit(solution)/shard_map/all_gather | solution.py:72
  8.0 272.9 %all-gather.8.cloned.1.call-start = ((), (), s32[]{:S(2)}) async-start(), calls=%async_computation.3 | async-start | bytes 5242880 | tf_op jit(solution)/shard_map/all_gather | solution.py:12
  147.7 198.0 %all-reduce.2.cloned.1.call-start = ((), (), s32[]{:S(2)}) async-start(), calls=%async_computation.1 | async-start | bytes 4194304 | tf_op jit(solution)/shard_map/psum | solution.py:63
  147.8 2.5 copy-start.2
  280.9 66.0 %copy-start.5 = (f32[128]{0:T(128)S(1)}, f32[128]{0:T(128)}, u32[]{:S(2)}) copy-start(f32[128]{0:T(128)} %param.17) | copy-start | bytes 1540
  280.9 67.2 %copy-start.3 = (bf16[1024,128]{1,0:T(8,128)(2,1)S(1)}, bf16[1024,128]{1,0:T(8,128)(2,1)}, u32[]{:S(2)}) copy-start(bf16[1024,128]{1,0:T(8,128)(2,1)} %param.12) | copy-start | bytes 786436
  280.9 67.2 %copy-start.6 = (bf16[128,128]{1,0:T(8,128)(2,1)S(1)}, bf16[128,128]{1,0:T(8,128)(2,1)}, u32[]{:S(2)}) copy-start(bf16[128,128]{1,0:T(8,128)(2,1)} %param.19) | copy-start | bytes 98308
Sparse Core Ops, SparseCore 0:
  8.9 31.8 all-gather.5
  42.7 25.8 all-gather.3
  147.8 52.0 all-gather.7
  281.0 64.6 all-reduce.1
